TPU v7x, 32 devices: a whole 2x2x4 slice. The times are simulated.
32 devices in a mesh: groups: 2 (over y), blk: 8 (over z, x), heads: 2 (over core).
Axes of the slice: x: 2, y: 2, z: 4, core: 2. Of those that a mesh axis runs over, the one named last changes fastest.
Arguments:
- queries: bfloat16 [16, 64, 128], P(('groups', 'blk'), 'heads'), parts along dimension 0, may hold values from -256 to 256
- prefix_keys: bfloat16 [4096, 8, 128], P(('groups', 'blk'), 'heads'), parts along dimension 0, may hold values from -12 to 12
- prefix_values: bfloat16 [4096, 8, 128], P(('groups', 'blk'), 'heads'), parts along dimension 0, may hold values from -12 to 12
- suffix_pool: bfloat16 [48, 2, 16, 8, 128], P(('groups', 'blk'), None, None, 'heads'), parts along dimension 0, may hold values from -8.375 to 8.375
- page_owner: int32 [6, 8], P('groups'), parts along dimension 0, may hold values from 0 to 7, as said below
- page_slot: int32 [6, 8], P('groups'), parts along dimension 0, may hold values from 0 to 2, as said below
- suffix_len: int32 [6], P('groups'), parts along dimension 0, may hold values from 1 to 128, as said below
- row_request: int32 [16], P('groups'), parts along dimension 0, may hold values from 0 to 2, as said below
Outputs:
- attn_out: bfloat16 [16, 64, 128], P(('groups', 'blk'), 'heads'), parts along dimension 0
There are 2 independent parts, one for each index of `groups`. A program takes and returns all parts, laid end to end along the dimension named above; each array names one. Nothing has to cross between parts.
Inputs may be any that keep to these rules, and one draw needn't show every extreme that they name: `row_request`: rows 0 to 5 belong to one request, whose last 6 suffix tokens they are, in order; each later row is the only row of its request; every request has rows. `suffix_len`: counts the rows' own tokens; the prefill span's request has 6 or more, and some other request has exactly 128. Each request has one page on every blk index: page j lies on (page_owner[r, 0] + j) modulo the number of blk indices. `page_slot`: A local slot of the owner's pool; two requests never share a slot on one owner.
All inputs are finite; a program needn't handle non-finite values.
Results may differ from a plain program's by a relative error of at most 0.005.
Values may be sent and summed in bfloat16 or wider, within the bound.
A program may use at most 64 MiB of HBM per device.

v0:
```python
import math
import jax
import jax.numpy as jnp
from jax import lax
from jax.sharding import PartitionSpec as P


def merge_parts(first, second):
    first_max, first_sum, first_acc = first
    second_max, second_sum, second_acc = second
    highest = jnp.maximum(first_max, second_max)
    first_weight = jnp.exp(first_max - highest)
    second_weight = jnp.exp(second_max - highest)
    return (
        highest,
        first_sum * first_weight + second_sum * second_weight,
        first_acc * first_weight[..., None] + second_acc * second_weight[..., None],
    )


def prefix_part(query_rows, prefix_keys, prefix_values, kblock):
    row_count, qheads, head_dim = query_rows.shape
    kv_heads = prefix_keys.shape[1]
    group = qheads // kv_heads
    score_scale = 1.0 / math.sqrt(head_dim)
    grouped = query_rows.reshape(row_count, kv_heads, group, head_dim)
    block_total = prefix_keys.shape[0] // kblock
    key_blocks = prefix_keys.reshape(block_total, kblock, kv_heads, head_dim)
    value_blocks = prefix_values.reshape(block_total, kblock, kv_heads, head_dim)

    def key_step(running, blocks):
        run_max, run_sum, run_acc = running
        key_blk, value_blk = blocks
        scores = (
            jnp.einsum("rgqd,kgd->rgqk", grouped, key_blk, preferred_element_type=jnp.float32)
            * score_scale
        )
        new_max = jnp.maximum(run_max, jnp.max(scores, axis=-1))
        rescale = jnp.exp(run_max - new_max)
        probs = jnp.exp(scores - new_max[..., None])
        run_sum = run_sum * rescale + jnp.sum(probs, axis=-1)
        run_acc = run_acc * rescale[..., None] + jnp.einsum(
            "rgqk,kgd->rgqd",
            probs.astype(jnp.bfloat16),
            value_blk,
            preferred_element_type=jnp.float32,
        )
        return ((new_max, run_sum, run_acc), None)

    initial = (
        jnp.full((row_count, kv_heads, group), -1e30, jnp.float32),
        jnp.zeros((row_count, kv_heads, group), jnp.float32),
        jnp.zeros((row_count, kv_heads, group, head_dim), jnp.float32),
    )
    (run_max, run_sum, run_acc), _ = lax.scan(key_step, initial, (key_blocks, value_blocks))
    return (
        run_max.reshape(row_count, qheads),
        run_sum.reshape(row_count, qheads),
        run_acc.reshape(row_count, qheads, head_dim),
    )


def paged_part(query_rows, page_keys, page_values, visible):
    row_count, qheads, head_dim = query_rows.shape
    kv_heads = page_keys.shape[2]
    group = qheads // kv_heads
    score_scale = 1.0 / math.sqrt(head_dim)
    grouped = query_rows.reshape(row_count, kv_heads, group, head_dim)
    scores = (
        jnp.einsum("rgqd,rkgd->rgqk", grouped, page_keys, preferred_element_type=jnp.float32)
        * score_scale
    )
    shown = visible[:, None, None, :]
    scores = jnp.where(shown, scores, -1e30)
    highest = jnp.max(scores, axis=-1)
    probs = jnp.where(shown, jnp.exp(scores - highest[..., None]), 0.0)
    totals = jnp.sum(probs, axis=-1)
    mixed = jnp.einsum(
        "rgqk,rkgd->rgqd",
        probs.astype(jnp.bfloat16),
        page_values,
        preferred_element_type=jnp.float32,
    )
    return (
        highest.reshape(row_count, qheads),
        totals.reshape(row_count, qheads),
        mixed.reshape(row_count, qheads, head_dim),
    )


def on_device(
    queries, prefix_keys, prefix_values, suffix_pool, page_owner, page_slot, suffix_len, row_request
):
    block_count = lax.axis_size("blk")
    self_index = lax.axis_index("blk")
    rows_dev, qheads, head_dim = queries.shape
    page_len = suffix_pool.shape[2]
    row_count = row_request.shape[0]
    req_count = suffix_len.shape[0]
    kblock = min(prefix_keys.shape[0], 256)
    row_order = jnp.arange(row_count, dtype=jnp.int32)
    same_req = row_request[:, None] == row_request[None, :]
    later_rows = jnp.sum(
        (same_req & (row_order[None, :] > row_order[:, None])).astype(jnp.int32), axis=1
    )
    one_hot = (row_request[:, None] == jnp.arange(req_count, dtype=jnp.int32)[None, :]).astype(
        jnp.int32
    )
    limits = jnp.sum(one_hot * suffix_len[None, :], axis=1) - later_rows
    home_owner = jnp.sum(one_hot * page_owner[None, :, 0], axis=1)
    own_slot = jnp.sum(jnp.where(page_owner == self_index, page_slot, 0), axis=1)
    row_slot = jnp.sum(one_hot * own_slot[None, :], axis=1)
    page_index = (self_index - home_owner) % block_count
    all_rows = lax.all_gather(queries, "blk", axis=0, tiled=True)
    partial_value = prefix_part(all_rows, prefix_keys, prefix_values, kblock)
    first_token = page_index * page_len
    page_data = suffix_pool[row_slot]
    visible = (
        first_token[:, None] + jnp.arange(page_len, dtype=jnp.int32)[None, :] < limits[:, None]
    )
    partial_value = merge_parts(
        partial_value, paged_part(all_rows, page_data[:, 0], page_data[:, 1], visible)
    )
    sectioned = (
        partial_value[0].reshape(block_count, rows_dev, qheads),
        partial_value[1].reshape(block_count, rows_dev, qheads),
        partial_value[2].reshape(block_count, rows_dev, qheads, head_dim),
    )
    part_max = lax.all_to_all(sectioned[0], "blk", split_axis=0, concat_axis=0, tiled=True)
    part_sum = lax.all_to_all(sectioned[1], "blk", split_axis=0, concat_axis=0, tiled=True)
    part_acc = lax.all_to_all(sectioned[2], "blk", split_axis=0, concat_axis=0, tiled=True)
    highest = jnp.max(part_max, axis=0)
    weight = jnp.exp(part_max - highest[None])
    return (
        jnp.sum(part_acc * weight[..., None], axis=0)
        / jnp.sum(part_sum * weight, axis=0)[..., None]
    ).astype(jnp.bfloat16)


def solution(mesh):
    placed = (
        P(("groups", "blk"), "heads", None),
        P(("groups", "blk"), "heads", None),
        P(("groups", "blk"), "heads", None),
        P(("groups", "blk"), None, None, "heads", None),
        P("groups", None),
        P("groups", None),
        P("groups"),
        P("groups"),
    )
    return jax.shard_map(
        on_device,
        mesh=mesh,
        in_specs=placed,
        out_specs=P(("groups", "blk"), "heads", None),
        check_vma=False,
    )
```

profile of v0, /device:TPU:0, one launch (start us, length us, event | category | flops | bytes accessed | tf_op | source)
XLA Modules:
  0.0 72.5 jit_solution(9709522602568486579)
XLA Ops:
  0.0 0.0 copy-start
  0.0 0.0 copy-start.3
  0.0 0.7 copy-done.3
  0.7 0.0 copy-start.5
  0.7 0.0 copy-start.4
  0.7 0.1 slice_reduce_fusion
  0.8 0.5 copy-done.5
  1.4 0.2 convert_reduce_fusion
  1.6 0.0 copy-done.4
  1.6 0.0 copy-start.6
  1.6 0.1 select_reduce_fusion.1
  1.7 0.5 copy-done.6
  2.2 0.1 select_reduce_fusion.3
  2.4 1.7 %gather_fusion = bf16[8,2,16,4,128]{4,3,2,1,0:T(4,128)(2,1)S(1)} fusion(bf16[3,2,16,4,128]{4,3,2,1,0:T(4,128)(2,1)} %param.11, s32[1024]{0:T(1024)S(1)} %pad_clamp_fusion), kind=kCustom, calls=%fused_computation | custom fusion | bytes 524320 | tf_op jit(solution)/shard_map/gather | solution.py:117
  4.0 0.0 copy-start.2
  4.0 0.1 fusion.29
  4.1 0.6 copy-done.2
  4.7 32.3 %all_gather.3 = bf16[8,32,128]{2,1,0:T(8,128)(2,1)S(1)} all-gather(bf16[1,32,128]{2,1,0:T(8,128)(2,1)S(1)} %copy-done.2), channel_id=1, replica_groups=mesh['groups'=2,'blk'=8,'heads'=2] {'blk'}, dimensions={0}, use_global_device_ids=true | all-gather | bytes 73728 | tf_op jit(solution)/shard_map/all_gather | solution.py:114
  37.1 0.1 add_compare_fusion
  37.1 0.0 copy-start.1
  37.1 0.3 fusion.31
  37.4 0.1 reshape.286
  37.5 0.2 fusion.13
  37.7 0.1 reshape.287
  37.8 0.3 copy-done.1
  38.1 0.3 fusion.30
  38.4 0.2 fusion.9
  38.6 0.1 reduce_sum.97
  38.7 0.1 max.64
  38.8 0.6 multiply_add_fusion
  39.4 5.5 %all-to-all-start.1 = ((f32[8,1,32]{2,1,0:T(1,128)}), f32[8,1,32]{2,1,0:T(1,128)S(1)}, u32[]{:S(2)}, u32[]{:S(2)}) async-start(f32[8,1,32]{2,1,0:T(1,128)} %bitcast.13), calls=%async_computation.1 | async-start | bytes 8192 | tf_op jit(solution)/shard_map/all_to_all | solution.py:129
  44.9 0.1 reshape.284
  45.0 0.1 max.62
  45.0 0.0 copy-done
  45.0 0.2 fusion.1
  45.3 6.1 %all-to-all-done.1 = f32[8,1,32]{2,1,0:T(1,128)S(1)} async-done(((f32[8,1,32]{2,1,0:T(1,128)}), f32[8,1,32]{2,1,0:T(1,128)S(1)}, u32[]{:S(2)}, u32[]{:S(2)}) %all-to-all-start.1) | async-done | bytes 1056 | tf_op jit(solution)/shard_map/all_to_all | solution.py:129
  51.4 3.3 %all-to-all-start.2 = ((f32[8,1,32]{2,1,0:T(1,128)}), f32[8,1,32]{2,1,0:T(1,128)S(1)}, u32[]{:S(2)}, u32[]{:S(2)}) async-start(f32[8,1,32]{2,1,0:T(1,128)} %bitcast.16), calls=%async_computation.2 | async-start | bytes 8192 | tf_op jit(solution)/shard_map/all_to_all | solution.py:130
  54.7 0.9 %fusion.6 = f32[8,1,32,128]{3,2,1,0:T(8,128)} fusion(bf16[8,1,16,4,128]{4,3,2,1,0:T(4,128)(2,1)S(1)} %get-tuple-element.34, f32[8,4,8,128]{3,2,0,1:T(8,128)S(1)} %fusion.1, f32[8,4,8,16]{3,2,1,0:T(8,128)S(1)} %get-tuple-element.42, f32[8,32]{1,0:T(8,128)S(1)} %get-tuple-element.38, f32[8,4,8]{2,1,0:T(4,128)S(1)} %get-tuple-element.41, ...), kind=kOutput, calls=%fused_computation.11 | convolution fusion | flops 1159168 | bytes 412800 | tf_op jit(solution)/shard_map/rgqk,rkgd->rgqd/dot_general | solution.py:78
  55.6 5.5 %all-to-all-done.2 = f32[8,1,32]{2,1,0:T(1,128)S(1)} async-done(((f32[8,1,32]{2,1,0:T(1,128)}), f32[8,1,32]{2,1,0:T(1,128)S(1)}, u32[]{:S(2)}, u32[]{:S(2)}) %all-to-all-start.2) | async-done | bytes 1056 | tf_op jit(solution)/shard_map/all_to_all | solution.py:130
  61.1 3.4 %all-to-all-start = ((f32[8,1,32,128]{3,2,1,0:T(8,128)}), f32[8,1,32,128]{3,2,1,0:T(8,128)S(1)}, u32[]{:S(2)}, u32[]{:S(2)}) async-start(f32[8,1,32,128]{3,2,1,0:T(8,128)} %fusion.6), calls=%async_computation | async-start | bytes 262144 | tf_op jit(solution)/shard_map/all_to_all | solution.py:131
  64.5 7.2 %all-to-all-done = f32[8,1,32,128]{3,2,1,0:T(8,128)S(1)} async-done(((f32[8,1,32,128]{3,2,1,0:T(8,128)}), f32[8,1,32,128]{3,2,1,0:T(8,128)S(1)}, u32[]{:S(2)}, u32[]{:S(2)}) %all-to-all-start) | async-done | bytes 131104 | tf_op jit(solution)/shard_map/all_to_all | solution.py:131
  71.7 0.1 multiply_reduce_fusion
  71.8 0.7 fusion.20
  (10 shorter events, 0.1 us)
Async XLA Ops:
  0.0 45.0 %copy-start = (bf16[256,4,128]{2,1,0:T(4,128)(2,1)S(1)}, bf16[256,4,128]{2,1,0:T(4,128)(2,1)}, u32[]{:S(2)}) copy-start(bf16[256,4,128]{2,1,0:T(4,128)(2,1)} %param.10) | copy-start | bytes 786436
  0.0 0.7 %copy-start.3 = (s32[3,8]{1,0:T(4,128)S(1)}, s32[3,8]{1,0:T(4,128)}, u32[]{:S(2)}) copy-start(s32[3,8]{1,0:T(4,128)} %param.12) | copy-start | bytes 292
  0.7 0.7 copy-start.5
  0.7 0.8 %copy-start.4 = (s32[3,8]{1,0:T(4,128)S(1)}, s32[3,8]{1,0:T(4,128)}, u32[]{:S(2)}) copy-start(s32[3,8]{1,0:T(4,128)} %param.13) | copy-start | bytes 292
  1.6 0.7 copy-start.6
  4.0 0.7 copy-start.2
  37.1 1.0 %copy-start.1 = (bf16[256,4,128]{2,1,0:T(4,128)(2,1)S(1)}, bf16[256,4,128]{2,1,0:T(4,128)(2,1)}, u32[]{:S(2)}) copy-start(bf16[256,4,128]{2,1,0:T(4,128)(2,1)} %param.9) | copy-start | bytes 786436
  39.4 12.0 %all-to-all-start.1 = ((f32[8,1,32]{2,1,0:T(1,128)}), f32[8,1,32]{2,1,0:T(1,128)S(1)}, u32[]{:S(2)}, u32[]{:S(2)}) async-start(f32[8,1,32]{2,1,0:T(1,128)} %bitcast.13), calls=%async_computation.1 | async-start | bytes 8192 | tf_op jit(solution)/shard_map/all_to_all | solution.py:129
  51.4 9.7 %all-to-all-start.2 = ((f32[8,1,32]{2,1,0:T(1,128)}), f32[8,1,32]{2,1,0:T(1,128)S(1)}, u32[]{:S(2)}, u32[]{:S(2)}) async-start(f32[8,1,32]{2,1,0:T(1,128)} %bitcast.16), calls=%async_computation.2 | async-start | bytes 8192 | tf_op jit(solution)/shard_map/all_to_all | solution.py:130
  61.1 10.7 %all-to-all-start = ((f32[8,1,32,128]{3,2,1,0:T(8,128)}), f32[8,1,32,128]{3,2,1,0:T(8,128)S(1)}, u32[]{:S(2)}, u32[]{:S(2)}) async-start(f32[8,1,32,128]{3,2,1,0:T(8,128)} %fusion.6), calls=%async_computation | async-start | bytes 262144 | tf_op jit(solution)/shard_map/all_to_all | solution.py:131
where the time goes:
time: 73 us; the launch traced here: 72.5 us
  blocking collectives  32.3 us (44%)
  waiting for transfers between devices  18.8 us (26%)
  starting transfers between devices  12.1 us (17%)
  local copies, waits for them, and re-layouts  5.05 us (7%)
  other arithmetic  2.39 us (3%)
  matrix products  1.66 us (2%)
    all_gather x1, blocking collectives, on_device(): all_rows = lax.all_gather(queries, 'blk', axis=0, tiled=True)  32.3 us
    all_to_all x1, waiting for transfers between devices, on_device(): lax.all_to_all(sectioned[2], 'blk', split_axis=0, concat_axis=0, tiled=True)  7.22 us
    all_to_all x1, waiting for transfers between devices, on_device(): lax.all_to_all(sectioned[0], 'blk', split_axis=0, concat_axis=0, tiled=True)  6.07 us
    all_to_all x1, waiting for transfers between devices, on_device(): lax.all_to_all(sectioned[1], 'blk', split_axis=0, concat_axis=0, tiled=True)  5.5 us
    all_to_all x1, starting transfers between devices, on_device(): lax.all_to_all(sectioned[0], 'blk', split_axis=0, concat_axis=0, tiled=True)  5.46 us
    all_to_all x1, starting transfers between devices, on_device(): lax.all_to_all(sectioned[2], 'blk', split_axis=0, concat_axis=0, tiled=True)  3.37 us
    all_to_all x1, starting transfers between devices, on_device(): lax.all_to_all(sectioned[1], 'blk', split_axis=0, concat_axis=0, tiled=True)  3.31 us
    unnamed x14, local copies, waits for them, and re-layouts  2.68 us
  transfers between devices with their start and end apart: 3, of which 3 were waited for; matrix products, arithmetic and copies ran while one was open for 2% of the time, Pallas kernels for 0%

commit v1 on v0

--- a/solution.py
+++ b/solution.py
@@ -111,7 +111,24 @@
     own_slot = jnp.sum(jnp.where(page_owner == self_index, page_slot, 0), axis=1)
     row_slot = jnp.sum(one_hot * own_slot[None, :], axis=1)
     page_index = (self_index - home_owner) % block_count
-    all_rows = lax.all_gather(queries, "blk", axis=0, tiled=True)
+    size, position, rows = (lax.axis_size("blk"), lax.axis_index("blk"), queries.shape[0])
+    right = [(i, (i + 1) % size) for i in range(size)]
+    left = [(i, (i - 1) % size) for i in range(size)]
+    whole = jnp.zeros((*queries.shape[:0], size * rows, *queries.shape[0 + 1 :]), queries.dtype)
+    whole = lax.dynamic_update_slice_in_dim(whole, queries, position * rows, axis=0)
+    from_left = from_right = queries
+    half = size // 2
+    for step in range(1, half + 1):
+        from_left = lax.ppermute(from_left, "blk", right)
+        whole = lax.dynamic_update_slice_in_dim(
+            whole, from_left, (position - step) % size * rows, axis=0
+        )
+        if step < size - half:
+            from_right = lax.ppermute(from_right, "blk", left)
+            whole = lax.dynamic_update_slice_in_dim(
+                whole, from_right, (position + step) % size * rows, axis=0
+            )
+    all_rows = whole
     partial_value = prefix_part(all_rows, prefix_keys, prefix_values, kblock)
     first_token = page_index * page_len
     page_data = suffix_pool[row_slot]

time: 73 us -> 68.1 us (0.933)
  blocking collectives: 32.3 us -> 0 us
  waiting for transfers between devices: 18.8 us -> 32.8 us
  starting transfers between devices: 12.1 us -> 25.7 us
    all_gather x1 -> x0, blocking collectives: 32.3 us -> none  [on_device(): all_rows = lax.all_gather(queries, 'blk', axis=0, tiled=True)]
    ppermute x0 -> x7, starting transfers between devices: none -> 15.7 us  [the longest x3 15.7 us: on_device(): from_right = lax.ppermute(from_right, 'blk', left)]
    ppermute x0 -> x7, waiting for transfers between devices: none -> 14 us  [the longest x4 12.6 us: on_device(): from_left = lax.ppermute(from_left, 'blk', right)]
    all_to_all x1, starting transfers between devices: 5.46 us -> 3.33 us  [on_device(): lax.all_to_all(sectioned[0], 'blk', split_axis=0, concat_axis=0, tiled=True)]
  transfers between devices with their start and end apart: 3 -> 10, of which waited for: 3 -> 6; matrix products, arithmetic and copies ran while one was open for 2% -> 5% of each run, Pallas kernels for 0% -> 0%
where the time goes in v1:
time: 68.1 us; the launch traced here: 67.6 us
  waiting for transfers between devices  32.8 us (48%)
  starting transfers between devices  25.7 us (38%)
  local copies, waits for them, and re-layouts  4.84 us (7%)
  other arithmetic  2.39 us (4%)
  matrix products  1.66 us (2%)
    ppermute x3, starting transfers between devices, on_device(): from_right = lax.ppermute(from_right, 'blk', left)  15.7 us
    ppermute x4, waiting for transfers between devices, on_device(): from_left = lax.ppermute(from_left, 'blk', right)  12.6 us
    all_to_all x1, waiting for transfers between devices, on_device(): lax.all_to_all(sectioned[2], 'blk', split_axis=0, concat_axis=0, tiled=True)  7.22 us
    all_to_all x1, waiting for transfers between devices, on_device(): lax.all_to_all(sectioned[0], 'blk', split_axis=0, concat_axis=0, tiled=True)  6.16 us
    all_to_all x1, waiting for transfers between devices, on_device(): lax.all_to_all(sectioned[1], 'blk', split_axis=0, concat_axis=0, tiled=True)  5.48 us
    all_to_all x1, starting transfers between devices, on_device(): lax.all_to_all(sectioned[2], 'blk', split_axis=0, concat_axis=0, tiled=True)  3.37 us
    all_to_all x1, starting transfers between devices, on_device(): lax.all_to_all(sectioned[0], 'blk', split_axis=0, concat_axis=0, tiled=True)  3.33 us
    all_to_all x1, starting transfers between devices, on_device(): lax.all_to_all(sectioned[1], 'blk', split_axis=0, concat_axis=0, tiled=True)  3.31 us
  transfers between devices with their start and end apart: 10, of which 6 were waited for; matrix products, arithmetic and copies ran while one was open for 5% of the time, Pallas kernels for 0%

profile of v1, /device:TPU:0, one launch (start us, length us, event | category | flops | bytes accessed | tf_op | source)
XLA Modules:
  0.0 67.6 jit_solution(10819442398684992052)
XLA Ops:
  0.0 0.0 copy-start
  0.0 6.0 %collective-permute-start.1 = (bf16[1,32,128]{2,1,0:T(8,128)(2,1)}, bf16[1,32,128]{2,1,0:T(8,128)(2,1)S(1)}, u32[]{:S(2)}, u32[]{:S(2)}) collective-permute-start(bf16[1,32,128]{2,1,0:T(8,128)(2,1)} %param.8), channel_id=1, source_target_pairs={{0,14},{2,0},{4,2},{6,4},{8,6},{10,8},{12,10},{14,12},{1,15},{3,1}... | collective-permute-start | bytes 24584 | tf_op jit(solution)/shard_map/ppermute | solution.py:127
  6.0 0.0 collective-permute-start
  6.0 0.0 copy-start.2
  6.0 0.0 copy-start.4
  6.0 0.7 %copy-done.2 = s32[3,8]{1,0:T(4,128)S(1)} copy-done((s32[3,8]{1,0:T(4,128)S(1)}, s32[3,8]{1,0:T(4,128)}, u32[]{:S(2)}) %copy-start.2) | copy-done | bytes 120
  6.7 0.1 slice_reduce_fusion
  6.8 0.0 copy-done.4
  6.8 0.0 copy-start.5
  6.8 0.1 select_reduce_fusion.1
  6.9 0.5 copy-done.5
  7.5 0.0 copy-start.6
  7.5 0.2 convert_reduce_fusion
  7.7 0.5 copy-done.6
  8.1 0.1 select_reduce_fusion.3
  8.3 1.7 %gather_fusion = bf16[8,2,16,4,128]{4,3,2,1,0:T(4,128)(2,1)S(1)} fusion(bf16[3,2,16,4,128]{4,3,2,1,0:T(4,128)(2,1)} %param.11, s32[1024]{0:T(1024)S(1)} %pad_clamp_fusion), kind=kCustom, calls=%fused_computation | custom fusion | bytes 524320 | tf_op jit(solution)/shard_map/gather | solution.py:134
  9.9 0.1 fusion.28
  10.0 0.1 add_compare_fusion
  10.1 0.0 copy-start.3
  10.1 0.7 %copy-done.3 = bf16[1,32,128]{2,1,0:T(8,128)(2,1)S(1)} copy-done((bf16[1,32,128]{2,1,0:T(8,128)(2,1)S(1)}, bf16[1,32,128]{2,1,0:T(8,128)(2,1)}, u32[]{:S(2)}) %copy-start.3) | copy-done | bytes 8216
  10.8 0.0 collective-permute-done.1
  10.8 4.7 %collective-permute-start.3 = (bf16[1,32,128]{2,1,0:T(8,128)(2,1)S(1)}, bf16[1,32,128]{2,1,0:T(8,128)(2,1)S(1)}, u32[]{:S(2)}, u32[]{:S(2)}) collective-permute-start(bf16[1,32,128]{2,1,0:T(8,128)(2,1)S(1)} %collective-permute-done.1), channel_id=1, source_target_pairs={{0,14},{2,0},{4,2},{6,4},{8,6},{10,8},{12,10},{14,12},{1,15},{3,1}... | collective-permute-start | bytes 24584 | tf_op jit(solution)/shard_map/ppermute | solution.py:127
  15.6 0.0 collective-permute-done
  15.6 0.0 collective-permute-start.2
  15.6 1.3 %collective-permute-done.3 = bf16[1,32,128]{2,1,0:T(8,128)(2,1)S(1)} collective-permute-done((bf16[1,32,128]{2,1,0:T(8,128)(2,1)S(1)}, bf16[1,32,128]{2,1,0:T(8,128)(2,1)S(1)}, u32[]{:S(2)}, u32[]{:S(2)}) %collective-permute-start.3) | collective-permute-done | bytes 8224 | tf_op jit(solution)/shard_map/ppermute | solution.py:127
  16.9 5.0 %collective-permute-start.5 = (bf16[1,32,128]{2,1,0:T(8,128)(2,1)S(1)}, bf16[1,32,128]{2,1,0:T(8,128)(2,1)S(1)}, u32[]{:S(2)}, u32[]{:S(2)}) collective-permute-start(bf16[1,32,128]{2,1,0:T(8,128)(2,1)S(1)} %collective-permute-done.3), channel_id=1, source_target_pairs={{0,14},{2,0},{4,2},{6,4},{8,6},{10,8},{12,10},{14,12},{1,15},{3,1}... | collective-permute-start | bytes 24584 | tf_op jit(solution)/shard_map/ppermute | solution.py:127
  21.9 0.0 collective-permute-done.2
  21.9 0.0 collective-permute-start.4
  21.9 6.3 %collective-permute-done.4 = bf16[1,32,128]{2,1,0:T(8,128)(2,1)S(1)} collective-permute-done((bf16[1,32,128]{2,1,0:T(8,128)(2,1)S(1)}, bf16[1,32,128]{2,1,0:T(8,128)(2,1)S(1)}, u32[]{:S(2)}, u32[]{:S(2)}) %collective-permute-start.4) | collective-permute-done | bytes 8224 | tf_op jit(solution)/shard_map/ppermute | solution.py:122
  28.3 0.0 collective-permute-start.6
  28.3 0.0 collective-permute-done.5
  28.3 6.3 %collective-permute-done.6 = bf16[1,32,128]{2,1,0:T(8,128)(2,1)S(1)} collective-permute-done((bf16[1,32,128]{2,1,0:T(8,128)(2,1)S(1)}, bf16[1,32,128]{2,1,0:T(8,128)(2,1)S(1)}, u32[]{:S(2)}, u32[]{:S(2)}) %collective-permute-start.6) | collective-permute-done | bytes 8224 | tf_op jit(solution)/shard_map/ppermute | solution.py:122
  34.6 0.3 fusion.30
  34.9 0.1 reshape.286
  35.0 0.1 reshape.284
  35.0 0.0 copy-done
  35.0 0.3 fusion.29
  35.4 0.1 max.64
  35.4 0.1 max.62
  35.5 0.0 copy-start.1
  35.5 0.2 fusion.12
  35.8 0.1 reshape.287
  35.8 0.2 fusion.8
  36.1 0.1 reduce_sum.97
  36.1 0.6 multiply_add_fusion
  36.8 3.3 %all-to-all-start.1 = ((f32[8,1,32]{2,1,0:T(1,128)}), f32[8,1,32]{2,1,0:T(1,128)S(1)}, u32[]{:S(2)}, u32[]{:S(2)}) async-start(f32[8,1,32]{2,1,0:T(1,128)} %bitcast.12), calls=%async_computation.1 | async-start | bytes 8192 | tf_op jit(solution)/shard_map/all_to_all | solution.py:146
  40.1 0.0 copy-done.1
  40.1 0.2 fusion.1
  40.4 6.2 %all-to-all-done.1 = f32[8,1,32]{2,1,0:T(1,128)S(1)} async-done(((f32[8,1,32]{2,1,0:T(1,128)}), f32[8,1,32]{2,1,0:T(1,128)S(1)}, u32[]{:S(2)}, u32[]{:S(2)}) %all-to-all-start.1) | async-done | bytes 1056 | tf_op jit(solution)/shard_map/all_to_all | solution.py:146
  46.5 3.3 %all-to-all-start.2 = ((f32[8,1,32]{2,1,0:T(1,128)}), f32[8,1,32]{2,1,0:T(1,128)S(1)}, u32[]{:S(2)}, u32[]{:S(2)}) async-start(f32[8,1,32]{2,1,0:T(1,128)} %bitcast.15), calls=%async_computation.2 | async-start | bytes 8192 | tf_op jit(solution)/shard_map/all_to_all | solution.py:147
  49.8 0.9 %fusion.5 = f32[8,1,32,128]{3,2,1,0:T(8,128)} fusion(bf16[8,1,16,4,128]{4,3,2,1,0:T(4,128)(2,1)S(1)} %get-tuple-element.34, f32[8,4,8,128]{3,2,0,1:T(8,128)S(1)} %fusion.1, f32[8,4,8,16]{3,2,1,0:T(8,128)S(1)} %get-tuple-element.42, f32[8,32]{1,0:T(8,128)S(1)} %get-tuple-element.38, f32[8,4,8]{2,1,0:T(4,128)S(1)} %get-tuple-element.41, ...), kind=kOutput, calls=%fused_computation.10 | convolution fusion | flops 1159168 | bytes 412800 | tf_op jit(solution)/shard_map/rgqk,rkgd->rgqd/dot_general | solution.py:78
  50.7 5.5 %all-to-all-done.2 = f32[8,1,32]{2,1,0:T(1,128)S(1)} async-done(((f32[8,1,32]{2,1,0:T(1,128)}), f32[8,1,32]{2,1,0:T(1,128)S(1)}, u32[]{:S(2)}, u32[]{:S(2)}) %all-to-all-start.2) | async-done | bytes 1056 | tf_op jit(solution)/shard_map/all_to_all | solution.py:147
  56.2 3.4 %all-to-all-start = ((f32[8,1,32,128]{3,2,1,0:T(8,128)}), f32[8,1,32,128]{3,2,1,0:T(8,128)S(1)}, u32[]{:S(2)}, u32[]{:S(2)}) async-start(f32[8,1,32,128]{3,2,1,0:T(8,128)} %fusion.5), calls=%async_computation | async-start | bytes 262144 | tf_op jit(solution)/shard_map/all_to_all | solution.py:148
  59.6 7.2 %all-to-all-done = f32[8,1,32,128]{3,2,1,0:T(8,128)S(1)} async-done(((f32[8,1,32,128]{3,2,1,0:T(8,128)}), f32[8,1,32,128]{3,2,1,0:T(8,128)S(1)}, u32[]{:S(2)}, u32[]{:S(2)}) %all-to-all-start) | async-done | bytes 131104 | tf_op jit(solution)/shard_map/all_to_all | solution.py:148
  66.9 0.1 multiply_reduce_fusion
  67.0 0.7 %fusion.19 = bf16[1,32,128]{2,1,0:T(8,128)(2,1)} fusion(f32[32,128]{1,0:T(8,128)S(1)} %multiply_reduce_fusion, f32[32]{0:T(128)S(1)} %get-tuple-element.20), kind=kLoop, calls=%fused_computation.29 | loop fusion | flops 8192 | bytes 24704 | tf_op jit(solution)/shard_map/convert_element_type | solution.py:154
  (19 shorter events, 0.2 us)
Async XLA Ops:
  0.0 35.0 %copy-start = (bf16[256,4,128]{2,1,0:T(4,128)(2,1)S(1)}, bf16[256,4,128]{2,1,0:T(4,128)(2,1)}, u32[]{:S(2)}) copy-start(bf16[256,4,128]{2,1,0:T(4,128)(2,1)} %param.9) | copy-start | bytes 786436
  0.0 10.8 %collective-permute-start.1 = (bf16[1,32,128]{2,1,0:T(8,128)(2,1)}, bf16[1,32,128]{2,1,0:T(8,128)(2,1)S(1)}, u32[]{:S(2)}, u32[]{:S(2)}) collective-permute-start(bf16[1,32,128]{2,1,0:T(8,128)(2,1)} %param.8), channel_id=1, source_target_pairs={{0,14},{2,0},{4,2},{6,4},{8,6},{10,8},{12,10},{14,12},{1,15},{3,1}... | collective-permute-start | bytes 24584 | tf_op jit(solution)/shard_map/ppermute | solution.py:127
  6.0 9.5 %collective-permute-start = (bf16[1,32,128]{2,1,0:T(8,128)(2,1)}, bf16[1,32,128]{2,1,0:T(8,128)(2,1)S(1)}, u32[]{:S(2)}, u32[]{:S(2)}) collective-permute-start(bf16[1,32,128]{2,1,0:T(8,128)(2,1)} %param.8), channel_id=1, source_target_pairs={{0,2},{2,4},{4,6},{6,8},{8,10},{10,12},{12,14},{14,0},{1,3},{3,5},... | collective-permute-start | bytes 24584 | tf_op jit(solution)/shard_map/ppermute | solution.py:122
  6.0 0.7 %copy-start.2 = (s32[3,8]{1,0:T(4,128)S(1)}, s32[3,8]{1,0:T(4,128)}, u32[]{:S(2)}) copy-start(s32[3,8]{1,0:T(4,128)} %param.12) | copy-start | bytes 292
  6.0 0.8 %copy-start.4 = (s32[3,8]{1,0:T(4,128)S(1)}, s32[3,8]{1,0:T(4,128)}, u32[]{:S(2)}) copy-start(s32[3,8]{1,0:T(4,128)} %param.13) | copy-start | bytes 292
  6.8 0.7 copy-start.5
  7.5 0.7 copy-start.6
  10.1 0.7 %copy-start.3 = (bf16[1,32,128]{2,1,0:T(8,128)(2,1)S(1)}, bf16[1,32,128]{2,1,0:T(8,128)(2,1)}, u32[]{:S(2)}) copy-start(bf16[1,32,128]{2,1,0:T(8,128)(2,1)} %param.8) | copy-start | bytes 24580
  10.8 6.1 %collective-permute-start.3 = (bf16[1,32,128]{2,1,0:T(8,128)(2,1)S(1)}, bf16[1,32,128]{2,1,0:T(8,128)(2,1)S(1)}, u32[]{:S(2)}, u32[]{:S(2)}) collective-permute-start(bf16[1,32,128]{2,1,0:T(8,128)(2,1)S(1)} %collective-permute-done.1), channel_id=1, source_target_pairs={{0,14},{2,0},{4,2},{6,4},{8,6},{10,8},{12,10},{14,12},{1,15},{3,1}... | collective-permute-start | bytes 24584 | tf_op jit(solution)/shard_map/ppermute | solution.py:127
  15.6 6.3 %collective-permute-start.2 = (bf16[1,32,128]{2,1,0:T(8,128)(2,1)S(1)}, bf16[1,32,128]{2,1,0:T(8,128)(2,1)S(1)}, u32[]{:S(2)}, u32[]{:S(2)}) collective-permute-start(bf16[1,32,128]{2,1,0:T(8,128)(2,1)S(1)} %collective-permute-done), channel_id=1, source_target_pairs={{0,2},{2,4},{4,6},{6,8},{8,10},{10,12},{12,14},{14,0},{1,3},{3,5},... | collective-permute-start | bytes 24584 | tf_op jit(solution)/shard_map/ppermute | solution.py:122
  16.9 11.3 %collective-permute-start.5 = (bf16[1,32,128]{2,1,0:T(8,128)(2,1)S(1)}, bf16[1,32,128]{2,1,0:T(8,128)(2,1)S(1)}, u32[]{:S(2)}, u32[]{:S(2)}) collective-permute-start(bf16[1,32,128]{2,1,0:T(8,128)(2,1)S(1)} %collective-permute-done.3), channel_id=1, source_target_pairs={{0,14},{2,0},{4,2},{6,4},{8,6},{10,8},{12,10},{14,12},{1,15},{3,1}... | collective-permute-start | bytes 24584 | tf_op jit(solution)/shard_map/ppermute | solution.py:127
  21.9 6.3 %collective-permute-start.4 = (bf16[1,32,128]{2,1,0:T(8,128)(2,1)S(1)}, bf16[1,32,128]{2,1,0:T(8,128)(2,1)S(1)}, u32[]{:S(2)}, u32[]{:S(2)}) collective-permute-start(bf16[1,32,128]{2,1,0:T(8,128)(2,1)S(1)} %collective-permute-done.2), channel_id=1, source_target_pairs={{0,2},{2,4},{4,6},{6,8},{8,10},{10,12},{12,14},{14,0},{1,3},{3,5},... | collective-permute-start | bytes 24584 | tf_op jit(solution)/shard_map/ppermute | solution.py:122
  28.3 6.3 %collective-permute-start.6 = (bf16[1,32,128]{2,1,0:T(8,128)(2,1)S(1)}, bf16[1,32,128]{2,1,0:T(8,128)(2,1)S(1)}, u32[]{:S(2)}, u32[]{:S(2)}) collective-permute-start(bf16[1,32,128]{2,1,0:T(8,128)(2,1)S(1)} %collective-permute-done.4), channel_id=1, source_target_pairs={{0,2},{2,4},{4,6},{6,8},{8,10},{10,12},{12,14},{14,0},{1,3},{3,5},... | collective-permute-start | bytes 24584 | tf_op jit(solution)/shard_map/ppermute | solution.py:122
  35.5 4.6 %copy-start.1 = (bf16[256,4,128]{2,1,0:T(4,128)(2,1)S(1)}, bf16[256,4,128]{2,1,0:T(4,128)(2,1)}, u32[]{:S(2)}) copy-start(bf16[256,4,128]{2,1,0:T(4,128)(2,1)} %param.10) | copy-start | bytes 786436
  36.8 9.8 %all-to-all-start.1 = ((f32[8,1,32]{2,1,0:T(1,128)}), f32[8,1,32]{2,1,0:T(1,128)S(1)}, u32[]{:S(2)}, u32[]{:S(2)}) async-start(f32[8,1,32]{2,1,0:T(1,128)} %bitcast.12), calls=%async_computation.1 | async-start | bytes 8192 | tf_op jit(solution)/shard_map/all_to_all | solution.py:146
  46.5 9.7 %all-to-all-start.2 = ((f32[8,1,32]{2,1,0:T(1,128)}), f32[8,1,32]{2,1,0:T(1,128)S(1)}, u32[]{:S(2)}, u32[]{:S(2)}) async-start(f32[8,1,32]{2,1,0:T(1,128)} %bitcast.15), calls=%async_computation.2 | async-start | bytes 8192 | tf_op jit(solution)/shard_map/all_to_all | solution.py:147
  56.2 10.7 %all-to-all-start = ((f32[8,1,32,128]{3,2,1,0:T(8,128)}), f32[8,1,32,128]{3,2,1,0:T(8,128)S(1)}, u32[]{:S(2)}, u32[]{:S(2)}) async-start(f32[8,1,32,128]{3,2,1,0:T(8,128)} %fusion.5), calls=%async_computation | async-start | bytes 262144 | tf_op jit(solution)/shard_map/all_to_all | solution.py:148
